TPU v7x, 32 devices: a whole 2x2x4 slice. The times are simulated.
32 devices in a mesh: row: 8 (over z, core), col: 4 (over y, x).
Axes of the slice: x: 2, y: 2, z: 4, core: 2. Of those that a mesh axis runs over, the one named last changes fastest.
Arguments:
- tiles: bfloat16 [4096, 128, 128], P(('row', 'col')), may hold values from -48 to 48
- tile_rows: int32 [4096], P(('row', 'col')), may hold values from 0 to 1023, as said below
- tile_cols: int32 [4096], P(('row', 'col')), may hold values from 0 to 1023, as said below
- tile_count: int32 [32], P(('row', 'col')), may hold values from 32 to 128, as said below
- degree: int32 [1024, 128], P(('row', 'col')), may hold values from 32 to 96
- labels: int32 [1024, 128], P(('row', 'col')), may hold values from 0 to 63
Outputs:
- scores: float32 [1024, 16, 128], P(('row', 'col'))
Inputs may be any that keep to these rules, and one draw needn't show every extreme that they name: tile_rows of the slots of device (r, c) lie in node-row blocks r * 128 to (r + 1) * 128 - 1. tile_cols of the slots of device (r, c) lie in node blocks (s * 4 + c) * 32 + o for some s below 8 and o below 32. `tile_count`: some device has all its slots live.
All inputs are finite; a program needn't handle non-finite values.
Results may differ from a plain program's by a relative error of at most 0.0039.
Values may be sent and summed in bfloat16 or wider, within the bound.
No kernel may reach another device: no remote copies, remote signals or barrier semaphores. Data moves between devices by JAX's collectives and lax.ppermute only.
A program may use at most 64 MiB of HBM per device.

v0:
```python
import jax
import jax.numpy as jnp
from jax import lax
from jax.sharding import PartitionSpec as P

QC = 16
ITERS = 2


def local(tiles, tile_rows, tile_cols, tile_count, degree, labels):
    ncol = lax.axis_size("col")
    row_pos = lax.axis_index("row")
    blk_dev = labels.shape[0]
    rblk = blk_dev * ncol
    scale = 1.0 / jnp.sqrt(degree.astype(jnp.float32))
    qidx = jnp.arange(QC, dtype=jnp.int32)
    prior = (labels[:, None, :] == qidx[None, :, None]).astype(jnp.float32)
    local_rows = tile_rows - row_pos * rblk
    owner = tile_cols // blk_dev
    local_cols = owner // ncol * blk_dev + tile_cols % blk_dev
    live = (jnp.arange(tiles.shape[0], dtype=jnp.int32) < tile_count[0]).astype(jnp.float32)
    field = prior
    for step in range(ITERS):
        if step == 0:
            own = (field * scale[:, None, :]).astype(jnp.bfloat16)
            gathered = lax.all_gather(own, "row", axis=0, tiled=True)
        else:
            own = (field * scale[:, None, :]).astype(jnp.bfloat16)
            gathered = lax.all_gather(own, "row", axis=0, tiled=True)
        picked = gathered[local_cols]
        terms = jnp.einsum("tqj,tij->tqi", picked, tiles, preferred_element_type=jnp.float32)
        terms = terms * live[:, None, None]
        partial_rows = jax.ops.segment_sum(terms, local_rows, num_segments=rblk)
        summed = lax.psum_scatter(partial_rows, "col", scatter_dimension=0, tiled=True)
        field = 0.8 * scale[:, None, :] * summed + 0.2 * prior
    return field


def solution(mesh):
    return jax.shard_map(
        local,
        mesh=mesh,
        in_specs=(
            P(("row", "col"), None, None),
            P(("row", "col")),
            P(("row", "col")),
            P(("row", "col")),
            P(("row", "col"), None),
            P(("row", "col"), None),
        ),
        out_specs=P(("row", "col"), None, None),
        check_vma=False,
    )
```

profile of v0, /device:TPU:0, one launch (start us, length us, event | category | flops | bytes accessed | tf_op | source)
XLA Modules:
  0.0 146.3 jit_solution(1190749417528610300)
XLA Ops:
  6.5 0.0 all-gather.3.cloned.1.call-start
  6.5 0.7 broadcast_multiply_fusion
  7.3 1.4 select_convert_fusion
  8.7 0.0 all-gather.3.cloned.1.call-update
  8.7 0.0 reduce-scatter.3.cloned.1.call-start
  9.4 0.7 compare_select_fusion
  10.1 0.7 broadcast_subtract_fusion
  10.8 23.0 %all-gather.3.cloned.1.call-done = bf16[256,16,128]{2,1,0:T(8,128)(2,1)} async-done(((bf16[32,16,128]{2,1,0:T(8,128)(2,1)}), bf16[256,16,128]{2,1,0:T(8,128)(2,1)}) %all-gather.3.cloned.1.call-update) | async-done | bytes 1048592 | tf_op jit(solution)/shard_map/all_gather | solution.py:26
  33.8 1.9 %gather_fusion = bf16[128,16,128]{2,1,0:T(8,128)(2,1)S(1)} fusion(bf16[256,16,128]{2,1,0:T(8,128)(2,1)} %all-gather.3.cloned.1.call-done, s32[1024]{0:T(1024)S(1)} %pad_clamp_fusion), kind=kCustom, calls=%fused_computation | custom fusion | bytes 1049088 | tf_op jit(solution)/shard_map/gather | solution.py:30
  35.7 0.0 copy-start.2
  35.7 4.5 %convolution_multiply_fusion.1 = f32[128,16,128]{2,1,0:T(8,128)S(1)} fusion(bf16[128,16,128]{2,1,0:T(8,128)(2,1)S(1)} %gather_fusion, bf16[128,128,128]{2,1,0:T(8,128)(2,1)} %param.6, f32[128]{0:T(128)S(1)} %compare_convert_fusion), kind=kOutput, calls=%fused_computation.5 | convolution fusion | flops 67371008 | bytes 5767680 | tf_op jit(solution)/shard_map/tqj,tij->tqi/dot_general | solution.py:31
  40.2 0.1 broadcast.42.clone
  40.3 5.2 %scatter_fusion = f32[128,16,128]{2,1,0:T(8,128)S(1)} fusion(f32[128,16,128]{2,1,0:T(8,128)S(1)} %broadcast.42.clone, s32[128]{0:T(128)S(1)} %broadcast_subtract_fusion, f32[128,16,128]{2,1,0:T(8,128)S(1)} %convolution_multiply_fusion.1), kind=kCustom, calls=%fused_computation.2 | custom fusion | flops 262144 | bytes 3146240 | tf_op jit(solution)/shard_map/scatter-add | solution.py:33
  45.5 0.0 copy-start.1
  45.5 1.0 copy-done.1
  46.4 0.0 reduce-scatter.3.cloned.1.call-update
  46.5 0.0 all-gather.5.cloned.1.call-start
  46.5 27.5 %reduce-scatter.3.cloned.1.call-done = f32[32,16,128]{2,1,0:T(8,128)} async-done(((f32[128,16,128]{2,1,0:T(8,128)}), f32[32,16,128]{2,1,0:T(8,128)}) %reduce-scatter.3.cloned.1.call-update) | async-done | bytes 262160 | tf_op jit(solution)/shard_map/reduce_scatter | solution.py:34
  74.0 0.0 copy-done.2
  74.0 1.7 %fusion.1 = bf16[32,16,128]{2,1,0:T(8,128)(2,1)} fusion(f32[32,16,128]{2,1,0:T(8,128)} %reduce-scatter.3.cloned.1.call-done, f32[32,128]{1,0:T(8,128)S(1)} %get-tuple-element.6, s32[32,128]{1,0:T(8,128)S(1)} %copy-done.2, f32[32,128]{1,0:T(8,128)S(1)} %get-tuple-element.5), kind=kLoop, calls=%fused_computation.9 | loop fusion | flops 393216 | bytes 442368 | tf_op jit(solution)/shard_map/convert_element_type | solution.py:28
  75.7 0.0 all-gather.5.cloned.1.call-update
  75.7 0.0 reduce-scatter.5.cloned.1.call-start
  75.7 22.2 %all-gather.5.cloned.1.call-done = bf16[256,16,128]{2,1,0:T(8,128)(2,1)} async-done(((bf16[32,16,128]{2,1,0:T(8,128)(2,1)}), bf16[256,16,128]{2,1,0:T(8,128)(2,1)}) %all-gather.5.cloned.1.call-update) | async-done | bytes 1048592 | tf_op jit(solution)/shard_map/all_gather | solution.py:29
  97.9 1.9 %gather_fusion.1 = bf16[128,16,128]{2,1,0:T(8,128)(2,1)S(1)} fusion(bf16[256,16,128]{2,1,0:T(8,128)(2,1)} %all-gather.5.cloned.1.call-done, s32[1024]{0:T(1024)S(1)} %pad_clamp_fusion), kind=kCustom, calls=%fused_computation.1 | custom fusion | bytes 1049088 | tf_op jit(solution)/shard_map/gather | solution.py:30
  99.9 4.5 %convolution_multiply_fusion = f32[128,16,128]{2,1,0:T(8,128)S(1)} fusion(bf16[128,16,128]{2,1,0:T(8,128)(2,1)S(1)} %gather_fusion.1, bf16[128,128,128]{2,1,0:T(8,128)(2,1)} %param.6, f32[128]{0:T(128)S(1)} %compare_convert_fusion), kind=kOutput, calls=%fused_computation.4 | convolution fusion | flops 67371008 | bytes 5767680 | tf_op jit(solution)/shard_map/tqj,tij->tqi/dot_general | solution.py:31
  104.3 0.1 broadcast.42
  104.4 5.2 %scatter_fusion.1 = f32[128,16,128]{2,1,0:T(8,128)S(1)} fusion(f32[128,16,128]{2,1,0:T(8,128)S(1)} %broadcast.42, s32[128]{0:T(128)S(1)} %broadcast_subtract_fusion, f32[128,16,128]{2,1,0:T(8,128)S(1)} %convolution_multiply_fusion), kind=kCustom, calls=%fused_computation.3 | custom fusion | flops 262144 | bytes 3146240 | tf_op jit(solution)/shard_map/scatter-add | solution.py:33
  109.6 0.0 copy-start
  109.6 1.0 copy-done
  110.6 0.0 reduce-scatter.5.cloned.1.call-update
  110.6 27.5 %reduce-scatter.5.cloned.1.call-done = f32[32,16,128]{2,1,0:T(8,128)} async-done(((f32[128,16,128]{2,1,0:T(8,128)}), f32[32,16,128]{2,1,0:T(8,128)}) %reduce-scatter.5.cloned.1.call-update) | async-done | bytes 262160 | tf_op jit(solution)/shard_map/reduce_scatter | solution.py:34
  138.1 1.7 %select_add_fusion = f32[32,16,128]{2,1,0:T(8,128)} fusion(f32[32,16,128]{2,1,0:T(8,128)} %reduce-scatter.5.cloned.1.call-done, s32[32,128]{1,0:T(8,128)S(1)} %copy-done.2, f32[32,128]{1,0:T(8,128)S(1)} %get-tuple-element.5), kind=kLoop, calls=%fused_computation.6 | loop fusion | flops 262144 | bytes 557056 | tf_op jit(solution)/shard_map/add | solution.py:35
  (2 shorter events, 0.0 us)
Async XLA Ops:
  6.5 27.3 %all-gather.3.cloned.1.call-start = ((), (), s32[]{:S(2)}) async-start(), calls=%async_computation.2 | async-start | bytes 1179648 | tf_op jit(solution)/shard_map/all_gather | solution.py:26
  8.7 65.3 %reduce-scatter.3.cloned.1.call-start = ((), (), s32[]{:S(2)}) async-start(), calls=%async_computation.3 | async-start | bytes 1310720 | tf_op jit(solution)/shard_map/reduce_scatter | solution.py:34
  35.7 38.3 %copy-start.2 = (s32[32,128]{1,0:T(8,128)S(1)}, s32[32,128]{1,0:T(8,128)}, u32[]{:S(2)}) copy-start(s32[32,128]{1,0:T(8,128)} %param.11) | copy-start | bytes 49156
  45.5 1.0 copy-start.1
  46.5 51.5 %all-gather.5.cloned.1.call-start = ((), (), s32[]{:S(2)}) async-start(), calls=%async_computation.4 | async-start | bytes 1179648 | tf_op jit(solution)/shard_map/all_gather | solution.py:29
  75.7 62.4 %reduce-scatter.5.cloned.1.call-start = ((), (), s32[]{:S(2)}) async-start(), calls=%async_computation.5 | async-start | bytes 1310720 | tf_op jit(solution)/shard_map/reduce_scatter | solution.py:34
  109.6 1.0 copy-start
Sparse Core Ops, SparseCore 0:
  9.0 24.7 all-gather.2
  46.6 27.3 reduce-scatter.2
  75.8 22.0 all-gather.4
  110.7 27.3 reduce-scatter.4
where the time goes:
time: 147 us; the launch traced here: 146 us
  waiting for transfers between devices  100 us (68%)
  other arithmetic  17.2 us (12%)
  between operations  13.9 us (9%)
  matrix products  8.93 us (6%)
  local copies, waits for them, and re-layouts  5.95 us (4%)
    reduce_scatter x2, waiting for transfers between devices, local(): lax.psum_scatter(partial_rows, 'col', scatter_dimension=0, tiled=True)  55 us
    all_gather x2, waiting for transfers between devices, local(): gathered = lax.all_gather(own, 'row', axis=0, tiled=True)  45.2 us
    scatter-add x2, other arithmetic, local(): partial_rows = jax.ops.segment_sum(terms, local_rows, num_segments=rblk)  10.3 us
    dot_general x2, matrix products, local(): jnp.einsum('tqj,tij->tqi', picked, tiles, preferred_element_type=jnp.floa...  8.93 us
    gather x2, local copies, waits for them, and re-layouts, local(): picked = gathered[local_cols]  3.85 us
    convert_element_type x2, other arithmetic, local(): own = (field * scale[:, None, :]).astype(jnp.bfloat16)  3.08 us
  transfers between devices with their start and end apart: 4, of which 4 were waited for; matrix products, arithmetic and copies ran while one was open for 1% of the time, Pallas kernels for 0%

commit v1 on v0

--- a/solution.py
+++ b/solution.py
@@ -5,6 +5,18 @@
 
 QC = 16
 ITERS = 2
+
+
+def gather_by_bits(x, axis, dim):
+    ways, here = (lax.axis_size(axis), lax.axis_index(axis))
+    grown, reach = (x, 1)
+    while reach < ways:
+        theirs = lax.ppermute(grown, axis, [(d, d ^ reach) for d in range(ways)])
+        mine_first = jnp.concatenate([grown, theirs], axis=dim)
+        theirs_first = jnp.concatenate([theirs, grown], axis=dim)
+        grown = jnp.where(here & reach == 0, mine_first, theirs_first)
+        reach = 2 * reach
+    return grown
 
 
 def local(tiles, tile_rows, tile_cols, tile_count, degree, labels):
@@ -26,7 +38,7 @@
             gathered = lax.all_gather(own, "row", axis=0, tiled=True)
         else:
             own = (field * scale[:, None, :]).astype(jnp.bfloat16)
-            gathered = lax.all_gather(own, "row", axis=0, tiled=True)
+            gathered = gather_by_bits(own, "row", 0)
         picked = gathered[local_cols]
         terms = jnp.einsum("tqj,tij->tqi", picked, tiles, preferred_element_type=jnp.float32)
         terms = terms * live[:, None, None]

time: 147 us -> 158 us (1.075)
  waiting for transfers between devices: 100 us -> 109 us
  starting transfers between devices: 0.13 us -> 4.19 us
    ppermute x0 -> x3, waiting for transfers between devices: none -> 31.1 us  [gather_by_bits(): theirs = lax.ppermute(grown, axis, [(d, d ^ reach) for d in range(ways)])]
    all_gather x2 -> x1, waiting for transfers between devices: 45.2 us -> 23 us  [local(): gathered = lax.all_gather(own, 'row', axis=0, tiled=True)]
    ppermute x0 -> x3, starting transfers between devices: none -> 4.1 us  [gather_by_bits(): theirs = lax.ppermute(grown, axis, [(d, d ^ reach) for d in range(ways)])]
  transfers between devices with their start and end apart: 4 -> 6, of which waited for: 4 -> 6; matrix products, arithmetic and copies ran while one was open for 1% -> 1% of each run, Pallas kernels for 0% -> 0%
where the time goes in v1:
time: 158 us
  waiting for transfers between devices  109 us (69%)
  other arithmetic  16.8 us (11%)
  between operations  13.9 us (9%)
  matrix products  8.93 us (6%)
  local copies, waits for them, and re-layouts  4.73 us (3%)
  starting transfers between devices  4.19 us (3%)
    reduce_scatter x2, waiting for transfers between devices, local(): lax.psum_scatter(partial_rows, 'col', scatter_dimension=0, tiled=True)  55.3 us
    ppermute x3, waiting for transfers between devices, gather_by_bits(): theirs = lax.ppermute(grown, axis, [(d, d ^ reach) for d in range(ways)])  31.1 us
    all_gather x1, waiting for transfers between devices, local(): gathered = lax.all_gather(own, 'row', axis=0, tiled=True)  23 us
    scatter-add x2, other arithmetic, local(): partial_rows = jax.ops.segment_sum(terms, local_rows, num_segments=rblk)  10.3 us
    dot_general x2, matrix products, local(): jnp.einsum('tqj,tij->tqi', picked, tiles, preferred_element_type=jnp.floa...  8.93 us
    ppermute x3, starting transfers between devices, gather_by_bits(): theirs = lax.ppermute(grown, axis, [(d, d ^ reach) for d in range(ways)])  4.1 us
  transfers between devices with their start and end apart: 6, of which 6 were waited for; matrix products, arithmetic and copies ran while one was open for 1% of the time, Pallas kernels for 0%

profile of v1, /device:TPU:0, one launch (start us, length us, event | category | flops | bytes accessed | tf_op | source)
XLA Modules:
  0.0 158.0 jit_solution(11974360401670630338)
XLA Ops:
  6.5 0.7 broadcast_multiply_fusion
  7.3 1.4 select_convert_fusion
  8.7 0.0 all-gather.2.cloned.1.call-update
  8.7 0.0 reduce-scatter.3.cloned.1.call-start
  9.4 0.7 compare_select_fusion
  10.1 0.7 broadcast_subtract_fusion
  10.8 23.0 %all-gather.2.cloned.1.call-done = bf16[256,16,128]{2,1,0:T(8,128)(2,1)} async-done(((bf16[32,16,128]{2,1,0:T(8,128)(2,1)}), bf16[256,16,128]{2,1,0:T(8,128)(2,1)}) %all-gather.2.cloned.1.call-update) | async-done | bytes 1048592 | tf_op jit(solution)/shard_map/all_gather | solution.py:38
  33.8 1.9 %gather_fusion = bf16[128,16,128]{2,1,0:T(8,128)(2,1)S(1)} fusion(bf16[256,16,128]{2,1,0:T(8,128)(2,1)} %all-gather.2.cloned.1.call-done, s32[1024]{0:T(1024)S(1)} %pad_clamp_fusion), kind=kCustom, calls=%fused_computation | custom fusion | bytes 1049088 | tf_op jit(solution)/shard_map/gather | solution.py:42
  35.7 4.5 %convolution_multiply_fusion.1 = f32[128,16,128]{2,1,0:T(8,128)S(1)} fusion(bf16[128,16,128]{2,1,0:T(8,128)(2,1)S(1)} %gather_fusion, bf16[128,128,128]{2,1,0:T(8,128)(2,1)} %param.6, f32[128]{0:T(128)S(1)} %compare_convert_fusion), kind=kOutput, calls=%fused_computation.5 | convolution fusion | flops 67371008 | bytes 5767680 | tf_op jit(solution)/shard_map/tqj,tij->tqi/dot_general | solution.py:43
  40.2 0.1 broadcast.44.clone
  40.3 5.2 %scatter_fusion = f32[128,16,128]{2,1,0:T(8,128)S(1)} fusion(f32[128,16,128]{2,1,0:T(8,128)S(1)} %broadcast.44.clone, s32[128]{0:T(128)S(1)} %broadcast_subtract_fusion, f32[128,16,128]{2,1,0:T(8,128)S(1)} %convolution_multiply_fusion.1), kind=kCustom, calls=%fused_computation.2 | custom fusion | flops 262144 | bytes 3146240 | tf_op jit(solution)/shard_map/scatter-add | solution.py:45
  45.5 1.0 copy-done.1
  46.4 0.0 reduce-scatter.3.cloned.1.call-update
  46.5 0.0 reduce-scatter.5.cloned.1.call-start
  46.5 27.5 %reduce-scatter.3.cloned.1.call-done = f32[32,16,128]{2,1,0:T(8,128)} async-done(((f32[128,16,128]{2,1,0:T(8,128)}), f32[32,16,128]{2,1,0:T(8,128)}) %reduce-scatter.3.cloned.1.call-update) | async-done | bytes 262160 | tf_op jit(solution)/shard_map/reduce_scatter | solution.py:46
  74.0 1.0 fusion.1
  75.0 0.1 collective-permute-start
  75.1 1.3 collective-permute-done
  76.4 1.6 collective-permute-start.1
  78.0 6.9 %collective-permute-done.1 = bf16[64,16,128]{2,1,0:T(8,128)(2,1)S(1)} collective-permute-done((bf16[64,16,128]{2,1,0:T(8,128)(2,1)S(1)}, bf16[64,16,128]{2,1,0:T(8,128)(2,1)S(1)}, u32[]{:S(2)}, u32[]{:S(2)}) %collective-permute-start.1) | collective-permute-done | bytes 262176 | tf_op jit(solution)/shard_map/ppermute | solution.py:14
  84.9 0.1 maximum_select_fusion.1
  85.0 2.5 %collective-permute-start.2 = (bf16[128,16,128]{2,1,0:T(8,128)(2,1)S(1)}, bf16[128,16,128]{2,1,0:T(8,128)(2,1)S(1)}, u32[]{:S(2)}, u32[]{:S(2)}) collective-permute-start(bf16[128,16,128]{2,1,0:T(8,128)(2,1)S(1)} %maximum_select_fusion.1), channel_id=1, source_target_pairs={{0,16},{4,20},{8,24},{12,28},{16,0},{20,4},{24,8},{28,12},{1,17},{... | collective-permute-start | bytes 1572872 | tf_op jit(solution)/shard_map/ppermute | solution.py:14
  87.4 22.9 %collective-permute-done.2 = bf16[128,16,128]{2,1,0:T(8,128)(2,1)S(1)} collective-permute-done((bf16[128,16,128]{2,1,0:T(8,128)(2,1)S(1)}, bf16[128,16,128]{2,1,0:T(8,128)(2,1)S(1)}, u32[]{:S(2)}, u32[]{:S(2)}) %collective-permute-start.2) | collective-permute-done | bytes 524320 | tf_op jit(solution)/shard_map/ppermute | solution.py:14
  110.3 0.2 maximum_select_fusion
  110.5 0.7 gather_fusion.1
  111.2 4.5 %convolution_multiply_fusion = f32[128,16,128]{2,1,0:T(8,128)S(1)} fusion(bf16[128,16,128]{2,1,0:T(8,128)(2,1)S(1)} %gather_fusion.1, bf16[128,128,128]{2,1,0:T(8,128)(2,1)} %param.6, f32[128]{0:T(128)S(1)} %compare_convert_fusion), kind=kOutput, calls=%fused_computation.4 | convolution fusion | flops 67371008 | bytes 5767680 | tf_op jit(solution)/shard_map/tqj,tij->tqi/dot_general | solution.py:43
  115.6 0.1 broadcast.44
  115.7 5.2 %scatter_fusion.1 = f32[128,16,128]{2,1,0:T(8,128)S(1)} fusion(f32[128,16,128]{2,1,0:T(8,128)S(1)} %broadcast.44, s32[128]{0:T(128)S(1)} %broadcast_subtract_fusion, f32[128,16,128]{2,1,0:T(8,128)S(1)} %convolution_multiply_fusion), kind=kCustom, calls=%fused_computation.3 | custom fusion | flops 262144 | bytes 3146240 | tf_op jit(solution)/shard_map/scatter-add | solution.py:45
  120.9 1.0 copy-done
  121.9 0.0 reduce-scatter.5.cloned.1.call-update
  121.9 27.9 %reduce-scatter.5.cloned.1.call-done = f32[32,16,128]{2,1,0:T(8,128)} async-done(((f32[128,16,128]{2,1,0:T(8,128)}), f32[32,16,128]{2,1,0:T(8,128)}) %reduce-scatter.5.cloned.1.call-update) | async-done | bytes 262160 | tf_op jit(solution)/shard_map/reduce_scatter | solution.py:46
  149.8 1.7 %select_add_fusion = f32[32,16,128]{2,1,0:T(8,128)} fusion(f32[32,16,128]{2,1,0:T(8,128)} %reduce-scatter.5.cloned.1.call-done, s32[32,128]{1,0:T(8,128)S(1)} %copy-done.2, f32[32,128]{1,0:T(8,128)S(1)} %get-tuple-element.5), kind=kLoop, calls=%fused_computation.8 | loop fusion | flops 262144 | bytes 557056 | tf_op jit(solution)/shard_map/add | solution.py:47
  (8 shorter events, 0.0 us)
Async XLA Ops:
  6.5 27.3 %all-gather.2.cloned.1.call-start = ((), (), s32[]{:S(2)}) async-start(), calls=%async_computation.2 | async-start | bytes 1179648 | tf_op jit(solution)/shard_map/all_gather | solution.py:38
  8.7 65.3 %reduce-scatter.3.cloned.1.call-start = ((), (), s32[]{:S(2)}) async-start(), calls=%async_computation.3 | async-start | bytes 1310720 | tf_op jit(solution)/shard_map/reduce_scatter | solution.py:46
  35.7 38.3 %copy-start.2 = (s32[32,128]{1,0:T(8,128)S(1)}, s32[32,128]{1,0:T(8,128)}, u32[]{:S(2)}) copy-start(s32[32,128]{1,0:T(8,128)} %param.11) | copy-start | bytes 49156
  45.5 1.0 copy-start.1
  46.5 103.3 %reduce-scatter.5.cloned.1.call-start = ((), (), s32[]{:S(2)}) async-start(), calls=%async_computation.4 | async-start | bytes 1310720 | tf_op jit(solution)/shard_map/reduce_scatter | solution.py:46
  75.0 1.4 collective-permute-start
  76.4 8.4 %collective-permute-start.1 = (bf16[64,16,128]{2,1,0:T(8,128)(2,1)S(1)}, bf16[64,16,128]{2,1,0:T(8,128)(2,1)S(1)}, u32[]{:S(2)}, u32[]{:S(2)}) collective-permute-start(bf16[64,16,128]{2,1,0:T(8,128)(2,1)S(1)} %maximum_select_fusion.2), channel_id=1, source_target_pairs={{0,8},{4,12},{8,0},{12,4},{16,24},{20,28},{24,16},{28,20},{1,9},{5... | collective-permute-start | bytes 786440 | tf_op jit(solution)/shard_map/ppermute | solution.py:14
  85.0 25.3 %collective-permute-start.2 = (bf16[128,16,128]{2,1,0:T(8,128)(2,1)S(1)}, bf16[128,16,128]{2,1,0:T(8,128)(2,1)S(1)}, u32[]{:S(2)}, u32[]{:S(2)}) collective-permute-start(bf16[128,16,128]{2,1,0:T(8,128)(2,1)S(1)} %maximum_select_fusion.1), channel_id=1, source_target_pairs={{0,16},{4,20},{8,24},{12,28},{16,0},{20,4},{24,8},{28,12},{1,17},{... | collective-permute-start | bytes 1572872 | tf_op jit(solution)/shard_map/ppermute | solution.py:14
  120.9 1.0 copy-start
Sparse Core Ops, SparseCore 0:
  9.0 24.7 all-gather.1
  46.6 27.3 reduce-scatter.2
  122.0 27.6 reduce-scatter.4
